TPU v7x, 128 devices: a whole 4x4x4 slice. The times are simulated.
128 devices in a mesh: dp: 64 (over z, y, x), tensor: 2 (over core).
Axes of the slice: x: 4, y: 4, z: 4, core: 2. Of those that a mesh axis runs over, the one named last changes fastest.
Arguments:
- queries: bfloat16 [2, 1024, 7, 4096], P(None, 'dp', None, 'tensor'), may hold values from -120 to 120
- new_kv: bfloat16 [2, 2, 1024, 7, 512], P(None, None, 'dp', None, 'tensor'), may hold values from -9 to 9
- kv_cache: bfloat16 [2, 1024, 512, 512], P(None, 'dp', None, 'tensor'), may hold values from -9 to 9
- context_len: int32 [1024], P('dp'), may hold values from 64 to 512, as said below
- accepted: int32 [2, 1024], replicated, may hold values from 0 to 6, as said below
- residual: bfloat16 [2, 1024, 7, 8192], P(None, 'dp', None, 'tensor'), may hold values from -25 to 25
- out_weight: bfloat16 [4096, 8192], P('tensor'), may hold values from -0.09375 to 0.09375
- draft_gain: float32 [8192], P('tensor'), may hold values from 0.1 to 1.9
- draft_weight: bfloat16 [8192, 1024], P('tensor'), may hold values from -0.0625 to 0.0625
Outputs:
- draft_kv: bfloat16 [2, 8192, 1024], P(None, 'dp', 'tensor')
Inputs may be any that keep to these rules, and one draw needn't show every extreme that they name: `context_len`: some conversation has exactly 512. `accepted`: in each step some conversation accepts all 6.
All inputs are finite; a program needn't handle non-finite values.
Results may differ from a plain program's by a relative error of at most 0.0025.
The roundings to bfloat16 on the way count: a program that leaves them out, or rounds other values in their place, can miss the bound.
Values may be sent and summed in bfloat16 or wider, within the bound.
A program may use at most 192 MiB of HBM per device.

v0:
```python
import jax
import jax.numpy as jnp
from jax import lax
from jax.sharding import PartitionSpec as P

HD = 128


def attend_block(query_rows, key_rows, value_rows, allowed, kv_local, group_size, head_dim):
    conversations = query_rows.shape[0]
    block_rows = query_rows.shape[1]
    key_count = key_rows.shape[1]
    queries_five = query_rows.reshape(conversations, block_rows, kv_local, group_size, head_dim)
    keys_four = key_rows.reshape(conversations, key_count, kv_local, head_dim)
    values_four = value_rows.reshape(conversations, key_count, kv_local, head_dim)
    scores = jnp.einsum(
        "cikgd,cnkd->ckgin", queries_five, keys_four, preferred_element_type=jnp.float32
    ) * head_dim ** (-0.5)
    scores = jnp.where(allowed[:, None, None], scores, -jnp.inf)
    maximum = jnp.max(scores, axis=-1, keepdims=True)
    expons = jnp.exp(scores - maximum)
    weights = (expons / jnp.sum(expons, axis=-1, keepdims=True)).astype(jnp.bfloat16)
    attended = jnp.einsum(
        "ckgin,cnkd->cikgd", weights, values_four, preferred_element_type=jnp.float32
    )
    return attended.astype(jnp.bfloat16).reshape(
        conversations * block_rows, kv_local * group_size * head_dim
    )


def draft_project(rows, draft_gain, draft_weight, width):
    hidden_wide = rows.astype(jnp.float32)
    square_part = jnp.sum(hidden_wide * hidden_wide, axis=-1)
    scaled = (hidden_wide * draft_gain[None, :]).astype(jnp.bfloat16)
    projected = jnp.dot(scaled, draft_weight, preferred_element_type=jnp.float32)
    squares_total = lax.psum(square_part, "tensor")
    own_heads = lax.psum_scatter(projected, "tensor", scatter_dimension=1, tiled=True)
    return (own_heads * lax.rsqrt(squares_total / width + 1e-05)[:, None]).astype(jnp.bfloat16)


def spread_rows(rows, dp_count, peer_rows):
    padded = jnp.pad(rows, ((0, dp_count * peer_rows - rows.shape[0]), (0, 0)))
    return padded.reshape(peer_rows, dp_count, rows.shape[1]).transpose(1, 0, 2)


def body(
    queries, new_kv, kv_cache, context_len, accepted, residual, out_weight, draft_gain, draft_weight
):
    dp_count = lax.axis_size("dp")
    dp_index = lax.axis_index("dp")
    steps_total = queries.shape[0]
    conv_local = queries.shape[1]
    block_rows = queries.shape[2]
    head_cols = queries.shape[3]
    cache_len = kv_cache.shape[2]
    kv_local = kv_cache.shape[3] // HD
    group_size = head_cols // HD // kv_local
    d_cols = residual.shape[3]
    width = out_weight.shape[1]
    row_total = conv_local * block_rows
    peer_rows = (row_total + dp_count - 1) // dp_count
    positions = jnp.arange(cache_len, dtype=jnp.int32)
    block_index = jnp.arange(block_rows, dtype=jnp.int32)
    causal = jnp.broadcast_to(
        block_index[None, :] <= block_index[:, None], (conv_local, block_rows, block_rows)
    )
    cache_allowed = jnp.broadcast_to(
        (positions[None, :] < context_len[:, None])[:, None, :], (conv_local, block_rows, cache_len)
    )
    own_accepted = lax.dynamic_slice_in_dim(accepted, dp_index * conv_local, conv_local, 1)
    slot_index = jnp.arange(peer_rows, dtype=jnp.int32)
    source_index = jnp.arange(dp_count, dtype=jnp.int32)
    row_number = slot_index * dp_count + dp_index
    row_valid = row_number < row_total
    row_clipped = jnp.minimum(row_number, row_total - 1)
    source_conv = source_index[:, None] * conv_local + (row_clipped // block_rows)[None, :]
    source_row = (row_clipped % block_rows)[None, :]
    outputs = []
    for step_index in range(steps_total):
        if step_index > 0:
            earlier_keys = new_kv[step_index - 1, 0]
            earlier_values = new_kv[step_index - 1, 1]
            earlier = own_accepted[step_index - 1]
        else:
            earlier_keys = jnp.zeros_like(new_kv[0, 0])
            earlier_values = jnp.zeros_like(new_kv[0, 1])
            earlier = jnp.full((conv_local,), -1, jnp.int32)
        old_allowed = jnp.broadcast_to(
            block_index[None, None, :] <= earlier[:, None, None],
            (conv_local, block_rows, block_rows),
        )
        allowed = jnp.concatenate([cache_allowed, old_allowed, causal], axis=2)
        key_rows = jnp.concatenate([kv_cache[0], earlier_keys, new_kv[step_index, 0]], axis=1)
        value_rows = jnp.concatenate([kv_cache[1], earlier_values, new_kv[step_index, 1]], axis=1)
        attended = attend_block(
            queries[step_index], key_rows, value_rows, allowed, kv_local, group_size, HD
        )
        partial_sum = jnp.dot(attended, out_weight, preferred_element_type=jnp.float32)
        summed = lax.psum_scatter(partial_sum, "tensor", scatter_dimension=1, tiled=True)
        hidden = (
            residual[step_index].reshape(row_total, d_cols).astype(jnp.float32) + summed
        ).astype(jnp.bfloat16)
        incoming = lax.all_to_all(
            spread_rows(hidden, dp_count, peer_rows), "dp", split_axis=0, concat_axis=0, tiled=True
        )
        new_rows = draft_project(
            incoming.reshape(dp_count * peer_rows, d_cols), draft_gain, draft_weight, width
        )
        limits = jnp.take(accepted[step_index], source_conv.reshape(-1), axis=0).reshape(
            dp_count, peer_rows
        )
        kept = jnp.logical_and(row_valid[None, :], source_row <= limits).reshape(
            dp_count * peer_rows
        )
        new_rows = jnp.where(kept[:, None], new_rows, jnp.zeros_like(new_rows))
        outputs.append(new_rows)
    return jnp.stack(outputs, axis=0)


def solution(mesh):
    in_specs = (
        P(None, "dp", None, "tensor"),
        P(None, None, "dp", None, "tensor"),
        P(None, "dp", None, "tensor"),
        P("dp"),
        P(),
        P(None, "dp", None, "tensor"),
        P("tensor", None),
        P("tensor"),
        P("tensor", None),
    )
    out_specs = P(None, "dp", "tensor")
    return jax.shard_map(body, mesh=mesh, in_specs=in_specs, out_specs=out_specs, check_vma=False)
```

profile of v0, /device:TPU:1, one launch (start us, length us, event | category | flops | bytes accessed | tf_op | source)
XLA Modules:
  0.0 211.8 jit_solution(16329647413635620509)
XLA Ops:
  9.1 5.8 %fusion.54 = (bf16[1,16,512,256]{3,2,1,0:T(8,128)(2,1)}, bf16[1,16,512,256]{3,2,1,0:T(8,128)(2,1)}) fusion(bf16[2,16,512,256]{3,2,1,0:T(8,128)(2,1)} %param.13), kind=kLoop, calls=%fused_computation.101 | loop fusion | bytes 16777216 | tf_op jit(solution)/shard_map/slice | solution.py:94
  14.9 6.4 %copy.37 = bf16[1,16,512,256]{2,3,1,0:T(8,128)(2,1)} copy(bf16[1,16,512,256]{3,2,1,0:T(8,128)(2,1)} %get-tuple-element.9) | data formatting | bytes 8388608
  21.3 6.5 %copy.17 = bf16[16,512,2,128]{3,1,2,0:T(8,128)(2,1)} copy(bf16[16,512,2,128]{1,3,2,0:T(8,128)(2,1)} %bitcast.114) | data formatting | bytes 8388608 | tf_op jit(solution)/shard_map/concatenate | solution.py:93
  27.9 6.4 %copy.36 = bf16[1,16,512,256]{2,3,1,0:T(8,128)(2,1)} copy(bf16[1,16,512,256]{3,2,1,0:T(8,128)(2,1)} %get-tuple-element.8) | data formatting | bytes 8388608
  34.3 6.4 %copy.14 = bf16[16,512,2,128]{3,1,2,0:T(8,128)(2,1)} copy(bf16[16,512,2,128]{1,3,2,0:T(8,128)(2,1)} %bitcast.115) | data formatting | bytes 8388608 | tf_op jit(solution)/shard_map/concatenate | solution.py:94
  41.0 4.1 %fusion.5 = f32[16,2,526,7,8]{2,4,3,1,0:T(8,128)S(1)} fusion(bf16[16,7,2,128]{3,1,2,0:T(8,128)(2,1)S(1)} %copy.18, bf16[16,512,2,128]{3,1,2,0:T(8,128)(2,1)} %copy.17, bf16[526]{0:T(1024)(128)(2,1)S(1)} %pad.27.clone, bf16[16,7,2,8,128]{4,3,2,0,1:T(8,128)(2,1)S(1)} %bitcast.120), kind=kOutput, calls=%fused_computation.15 | convolution fusion | flops 254230528 | bytes 8481820 | tf_op jit(solution)/shard_map/cikgd,cnkd->ckgin/dot_general | solution.py:16
  45.1 20.3 %fusion.59 = (f32[16,2,8,7]{2,3,1,0:T(8,128)S(1)}, f32[16,2,8,7,526]{4,2,3,1,0:T(8,128)S(1)}) fusion(f32[16,2,526,7,8]{2,4,3,1,0:T(8,128)S(1)} %fusion.5, pred[16,7,526]{2,1,0:T(8,128)(4,1)S(1)} %get-tuple-element.18), kind=kOutput, calls=%fused_computation.106 | output fusion | flops 5656077 | bytes 7606816 | tf_op jit(solution)/shard_map/sub | solution.py:21
  65.3 1.4 fusion.32
  67.0 14.8 %fusion.60 = f32[112,8192]{1,0:T(8,128)} fusion(bf16[112,2048]{1,0:T(8,128)(2,1)S(1)} %reshape.171, bf16[2048,8192]{1,0:T(8,128)(2,1)} %param.17), kind=kOutput, calls=%fused_computation.107 | convolution fusion | flops 3758096384 | bytes 37683200 | tf_op jit(solution)/shard_map/dot_general | solution.py:98
  82.4 3.5 %fusion.12 = f32[16,2,526,7,8]{2,4,3,1,0:T(8,128)S(1)} fusion(bf16[16,7,2,128]{3,1,2,0:T(8,128)(2,1)S(1)} %copy.28, bf16[16,7,2,128]{3,1,2,0:T(8,128)(2,1)S(1)} %copy.18, bf16[16,512,2,128]{3,1,2,0:T(8,128)(2,1)} %copy.17, bf16[16,7,2,8,128]{4,3,2,0,1:T(8,128)(2,1)S(1)} %bitcast.121), kind=kOutput, calls=%fused_computation.24 | convolution fusion | flops 254230528 | bytes 8538112 | tf_op jit(solution)/shard_map/cikgd,cnkd->ckgin/dot_general | solution.py:16
  85.8 20.3 %fusion.58 = (f32[16,2,8,7]{2,3,1,0:T(8,128)S(1)}, f32[16,2,8,7,526]{4,2,3,1,0:T(8,128)S(1)}) fusion(f32[16,2,526,7,8]{2,4,3,1,0:T(8,128)S(1)} %fusion.12, pred[16,7,526]{2,1,0:T(8,128)(4,1)S(1)} %get-tuple-element.19), kind=kOutput, calls=%fused_computation.105 | output fusion | flops 5656077 | bytes 7606816 | tf_op jit(solution)/shard_map/sub | solution.py:21
  106.1 1.4 fusion.33
  107.9 14.8 %fusion.61 = f32[112,8192]{1,0:T(8,128)} fusion(bf16[112,2048]{1,0:T(8,128)(2,1)S(1)} %reshape.173, bf16[2048,8192]{1,0:T(8,128)(2,1)} %param.17), kind=kOutput, calls=%fused_computation.108 | convolution fusion | flops 3758096384 | bytes 37683200 | tf_op jit(solution)/shard_map/dot_general | solution.py:98
  122.7 1.5 copy-done.2
  124.1 1.5 slice_convert_fusion.1
  126.8 1.5 reshape.175
  128.5 2.2 %add_convert_fusion.1 = bf16[112,4096]{1,0:T(8,128)(2,1)S(1)} fusion(f32[112,4096]{1,0:T(8,128)} %reshape.175, f32[112,4096]{1,0:T(8,128)} %reduce-scatter.5.cloned.1.call-done), kind=kLoop, calls=%fused_computation.47 | loop fusion | flops 917504 | bytes 4587520 | tf_op jit(solution)/shard_map/convert_element_type | solution.py:102
  130.9 2.1 copy.47
  132.9 12.0 %all-to-all-start = ((bf16[64,2,4096]{2,1,0:T(2,128)(2,1)}), bf16[64,2,4096]{2,1,0:T(2,128)(2,1)S(1)}, u32[]{:S(2)}, u32[]{:S(2)}) async-start(bf16[64,2,4096]{2,1,0:T(2,128)(2,1)} %bitcast.111), calls=%async_computation.1 | async-start | bytes 2097152 | tf_op jit(solution)/shard_map/all_to_all | solution.py:103
  144.9 2.6 %copy.22 = f32[1,16,7,4096]{3,2,1,0:T(8,128)S(1)} copy(f32[1,16,7,4096]{3,1,2,0:T(8,128)} %get-tuple-element.11) | data formatting | bytes 3670016 | tf_op jit(solution)/shard_map/convert_element_type | solution.py:101
  147.5 1.5 reshape.177
  149.0 2.2 %add_convert_fusion = bf16[112,4096]{1,0:T(8,128)(2,1)S(1)} fusion(f32[112,4096]{1,0:T(8,128)} %reshape.177, f32[112,4096]{1,0:T(8,128)} %reduce-scatter.9.cloned.1.call-done), kind=kLoop, calls=%fused_computation.46 | loop fusion | flops 917504 | bytes 4587520 | tf_op jit(solution)/shard_map/convert_element_type | solution.py:102
  151.4 2.1 copy.46
  153.5 9.1 %all-to-all-done = bf16[64,2,4096]{2,1,0:T(2,128)(2,1)S(1)} async-done(((bf16[64,2,4096]{2,1,0:T(2,128)(2,1)}), bf16[64,2,4096]{2,1,0:T(2,128)(2,1)S(1)}, u32[]{:S(2)}, u32[]{:S(2)}) %all-to-all-start) | async-done | bytes 1048608 | tf_op jit(solution)/shard_map/all_to_all | solution.py:103
  162.5 4.9 %all-to-all-start.1 = ((bf16[64,2,4096]{2,1,0:T(2,128)(2,1)}), bf16[64,2,4096]{2,1,0:T(2,128)(2,1)S(1)}, u32[]{:S(2)}, u32[]{:S(2)}) async-start(bf16[64,2,4096]{2,1,0:T(2,128)(2,1)} %bitcast.110), calls=%async_computation.4 | async-start | bytes 2097152 | tf_op jit(solution)/shard_map/all_to_all | solution.py:103
  167.5 1.5 reshape.176
  169.0 6.1 %fusion.34 = f32[128,1024]{1,0:T(8,128)} fusion(bf16[4096,1024]{1,0:T(8,128)(2,1)} %param.19, f32[128,4096]{1,0:T(8,128)} %reshape.176, f32[4096]{0:T(1024)S(1)} %copy-done.4), kind=kOutput, calls=%fused_computation.52 | convolution fusion | flops 1074790400 | bytes 11026432 | tf_op jit(solution)/shard_map/dot_general | solution.py:35
  177.5 6.5 %all-to-all-done.1 = bf16[64,2,4096]{2,1,0:T(2,128)(2,1)S(1)} async-done(((bf16[64,2,4096]{2,1,0:T(2,128)(2,1)}), bf16[64,2,4096]{2,1,0:T(2,128)(2,1)S(1)}, u32[]{:S(2)}, u32[]{:S(2)}) %all-to-all-start.1) | async-done | bytes 1048608 | tf_op jit(solution)/shard_map/all_to_all | solution.py:103
  184.0 1.5 reshape.178
  185.5 6.3 %fusion.35 = f32[128,1024]{1,0:T(8,128)} fusion(bf16[4096,1024]{1,0:T(8,128)(2,1)} %param.19, f32[128,4096]{1,0:T(8,128)} %reshape.178, f32[4096]{0:T(1024)S(1)} %copy-done.4), kind=kOutput, calls=%fused_computation.53 | convolution fusion | flops 1074790400 | bytes 11026432 | tf_op jit(solution)/shard_map/dot_general | solution.py:35
  194.5 5.2 %all-reduce.2 = (f32[128]{0:T(128)S(1)}, f32[128]{0:T(128)S(1)}) all-reduce(f32[128]{0:T(128)S(1)} %reduce_sum.45, f32[128]{0:T(128)S(1)} %reduce_sum.42), channel_id=1, replica_groups=mesh['dp'=64,'tensor'=2] {'tensor'}, use_global_device_ids=true, to_apply=%region_11.13 | all-reduce | flops 256 | bytes 2048 | tf_op jit(solution)/shard_map/psum | solution.py:36
  200.7 2.8 %reduce-scatter.11.cloned.1.call-done = f32[128,512]{1,0:T(8,128)} async-done(((f32[128,1024]{1,0:T(8,128)}), f32[128,512]{1,0:T(8,128)}) %reduce-scatter.11.cloned.1.call-update) | async-done | bytes 262160 | tf_op jit(solution)/shard_map/reduce_scatter | solution.py:37
  (77 shorter events, 13.3 us)
Async XLA Ops:
  6.5 122.0 %reduce-scatter.5.cloned.1.call-start = ((), (), s32[]{:S(2)}) async-start(), calls=%async_computation.6 | async-start | bytes 5505024 | tf_op jit(solution)/shard_map/reduce_scatter | solution.py:99
  21.3 6.5 %copy-start.3 = (bf16[2,16,7,2048]{3,1,2,0:T(8,128)(2,1)S(1)}, bf16[2,16,7,2048]{3,1,2,0:T(8,128)(2,1)}, u32[]{:S(2)}) copy-start(bf16[2,16,7,2048]{3,1,2,0:T(8,128)(2,1)} %param.11) | copy-start | bytes 2752516
  45.0 20.3 %copy-start = (bf16[16,512,2,128]{3,1,2,0:T(8,128)(2,1)S(1)}, bf16[16,512,2,128]{3,1,2,0:T(8,128)(2,1)}, u32[]{:S(2)}) copy-start(bf16[16,512,2,128]{3,1,2,0:T(8,128)(2,1)} %copy.14) | copy-start | bytes 12582916
  81.9 67.1 %reduce-scatter.9.cloned.1.call-start = ((), (), s32[]{:S(2)}) async-start(), calls=%async_computation.8 | async-start | bytes 5505024 | tf_op jit(solution)/shard_map/reduce_scatter | solution.py:99
  85.8 20.3 %copy-start.1 = (bf16[16,512,2,128]{3,1,2,0:T(8,128)(2,1)S(1)}, bf16[16,512,2,128]{3,1,2,0:T(8,128)(2,1)}, u32[]{:S(2)}) copy-start(bf16[16,512,2,128]{3,1,2,0:T(8,128)(2,1)} %copy.14) | copy-start | bytes 12582916
  122.6 1.5 copy-start.2
  132.9 29.6 %all-to-all-start = ((bf16[64,2,4096]{2,1,0:T(2,128)(2,1)}), bf16[64,2,4096]{2,1,0:T(2,128)(2,1)S(1)}, u32[]{:S(2)}, u32[]{:S(2)}) async-start(bf16[64,2,4096]{2,1,0:T(2,128)(2,1)} %bitcast.111), calls=%async_computation.1 | async-start | bytes 2097152 | tf_op jit(solution)/shard_map/all_to_all | solution.py:103
  151.3 17.7 %copy-start.4 = (f32[4096]{0:T(1024)S(1)}, f32[4096]{0:T(1024)}, u32[]{:S(2)}) copy-start(f32[4096]{0:T(1024)} %param.18) | copy-start | bytes 49156
  162.5 21.5 %all-to-all-start.1 = ((bf16[64,2,4096]{2,1,0:T(2,128)(2,1)}), bf16[64,2,4096]{2,1,0:T(2,128)(2,1)S(1)}, u32[]{:S(2)}, u32[]{:S(2)}) async-start(bf16[64,2,4096]{2,1,0:T(2,128)(2,1)} %bitcast.110), calls=%async_computation.4 | async-start | bytes 2097152 | tf_op jit(solution)/shard_map/all_to_all | solution.py:103
  167.4 32.3 %reduce-scatter.7.cloned.1.call-start = ((), (), s32[]{:S(2)}) async-start(), calls=%async_computation.7 | async-start | bytes 786432 | tf_op jit(solution)/shard_map/reduce_scatter | solution.py:37
  169.0 6.2 %copy-start.5 = (s32[2,1024]{1,0:T(2,128)S(1)}, s32[2,1024]{1,0:T(2,128)}, u32[]{:S(2)}) copy-start(s32[2,1024]{1,0:T(2,128)} %param.15) | copy-start | bytes 24580
  175.1 28.4 %reduce-scatter.11.cloned.1.call-start = ((), (), s32[]{:S(2)}) async-start(), calls=%async_computation.9 | async-start | bytes 786432 | tf_op jit(solution)/shard_map/reduce_scatter | solution.py:37
Sparse Core Ops, SparseCore 0:
  82.0 17.8 reduce-scatter.4
  122.8 17.8 reduce-scatter.8
  175.2 13.9 reduce-scatter.6
  192.0 11.4 reduce-scatter.10
where the time goes:
time: 213 us; the launch traced here: 212 us
  other arithmetic  52.8 us (25%)
  local copies, waits for them, and re-layouts  52.4 us (25%)
  matrix products  52.4 us (25%)
  waiting for transfers between devices  18.5 us (9%)
  starting transfers between devices  17.1 us (8%)
  between operations  13.6 us (6%)
  blocking collectives  5.16 us (2%)
    sub x2, other arithmetic, attend_block(): expons = jnp.exp(scores - maximum)  40.5 us
    dot_general x2, matrix products, body(): jnp.dot(attended, out_weight, preferred_element_type=jnp.float32)  29.6 us
    all_to_all x2, starting transfers between devices, body(): lax.all_to_all(spread_rows(hidden, dp_count, peer_rows), 'dp', split_axis...  16.8 us
    all_to_all x2, waiting for transfers between devices, body(): lax.all_to_all(spread_rows(hidden, dp_count, peer_rows), 'dp', split_axis...  15.6 us
    unnamed x16, local copies, waits for them, and re-layouts  14.4 us
    dot_general x2, matrix products, draft_project(): jnp.dot(scaled, draft_weight, preferred_element_type=jnp.float32)  12.4 us
    dot_general x2, matrix products, attend_block(): jnp.einsum('cikgd,cnkd->ckgin', queries_five, keys_four, preferred_elemen...  7.52 us
    convert_element_type x4, local copies, waits for them, and re-layouts, body(): residual[step_index].reshape(row_total, d_cols).astype(jnp.float32) + summed  6.68 us
  transfers between devices with their start and end apart: 6, of which 3 were waited for; matrix products, arithmetic and copies ran while one was open for 37% of the time, Pallas kernels for 0%

commit v1 on v0

v1 whole, which is shorter than its diff:
```python
import functools

import jax
import jax.numpy as jnp
from jax import lax
from jax.experimental import pallas as pl
from jax.experimental.pallas import tpu as pltpu
from jax.sharding import PartitionSpec as P

HD = 128
PADDED = 8
EXTRA = 128
SLOTS = 3
SENDS = 4
WIDE = 512
MESH = pl.DeviceIdType.MESH


def split_index(x, n):
    if n & (n - 1) == 0:
        shift = n.bit_length() - 1
        return x >> shift, x & (n - 1)
    if n == 7:
        top = (x * 9363) >> 16
        return top, x - top * n
    return x // n, x % n


def one_hot(have, want):
    return jnp.where(have == want, 1.0, 0.0).astype(jnp.bfloat16)


def fused_kernel(
    length_ref,
    accepted_ref,
    gain_ref,
    queries_hbm,
    new_kv_hbm,
    cache_hbm,
    residual_hbm,
    weight_hbm,
    draft_hbm,
    out_ref,
    row_v,
    pad_v,
    new_v,
    extra_v,
    k_v,
    v_v,
    hidden_v,
    weight_v,
    draft_v,
    spread_v,
    gather_v,
    perm_v,
    keep_v,
    send_v,
    recv_v,
    square_v,
    square_recv,
    ex_send,
    ex_recv,
    rows_v,
    packet_v,
    first_sem,
    pair_sem,
    weight_sem,
    draft_sem,
    send_sem,
    recv_sem,
    ex_send_sem,
    ex_recv_sem,
    row_send_sem,
    row_recv_sem,
    *,
    width,
    steps,
    conv,
    block,
):
    dp_count = out_ref.shape[0]
    ctx = cache_hbm.shape[2]
    head_cols = queries_hbm.shape[1]
    kv_local = cache_hbm.shape[3] // HD
    group = head_cols // HD // kv_local
    pairs = conv // 2
    chunks = recv_v.shape[0]
    step_rows = conv * block
    rows = steps * step_rows
    tall = steps * PADDED
    own_cols = draft_v.shape[2]
    quarters = own_cols // HD
    peer_rows = packet_v.shape[1] // (steps * quarters)
    me = lax.axis_index("dp")
    core = lax.axis_index("tensor")
    other = 1 - core

    def pair_copies(p):
        slot = lax.rem(p, SLOTS)
        span = pl.ds(p * 2, 2)
        return (
            pltpu.make_async_copy(
                cache_hbm.at[0, span], k_v.at[slot, :, pl.ds(0, ctx)], pair_sem.at[0, slot]
            ),
            pltpu.make_async_copy(
                cache_hbm.at[1, span], v_v.at[slot, :, pl.ds(0, ctx)], pair_sem.at[1, slot]
            ),
        )

    def weight_copy(c):
        side = jnp.where(c < chunks, other, core)
        at = pl.multiple_of(side * (chunks * WIDE) + lax.rem(c, chunks) * WIDE, WIDE)
        return pltpu.make_async_copy(
            weight_hbm.at[:, pl.ds(at, WIDE)], weight_v.at[c], weight_sem.at[c]
        )

    def draft_copy(half):
        side = other if half == 0 else core
        at = pl.multiple_of(side * own_cols, own_cols)
        return pltpu.make_async_copy(
            draft_hbm.at[:, pl.ds(at, own_cols)], draft_v.at[half], draft_sem.at[half]
        )

    query_copy = pltpu.make_async_copy(queries_hbm, row_v, first_sem.at[0])
    new_copy = pltpu.make_async_copy(new_kv_hbm, new_v, first_sem.at[1])
    residual_copy = pltpu.make_async_copy(residual_hbm, hidden_v, first_sem.at[2])
    query_copy.start()
    new_copy.start()
    for p in range(min(SLOTS - 1, pairs)):
        for copy in pair_copies(p):
            copy.start()

    barrier = pltpu.get_barrier_semaphore()
    pl.semaphore_signal(barrier, inc=1, device_id=(me, other), device_id_type=MESH)

    def greet(k, carry):
        pl.semaphore_signal(
            barrier, inc=1, device_id=(lax.rem(me + k, dp_count), core), device_id_type=MESH
        )
        return carry

    lax.fori_loop(1, dp_count, greet, 0)

    k_v[:, :, ctx + tall :, :] = jnp.zeros((SLOTS, 2, EXTRA - tall, kv_local * HD), jnp.bfloat16)
    v_v[:, :, ctx + tall :, :] = jnp.zeros((SLOTS, 2, EXTRA - tall, kv_local * HD), jnp.bfloat16)

    line = lax.broadcasted_iota(jnp.int32, (conv * tall, 1), 0)
    rest, place = split_index(line, PADDED)
    which, step = split_index(rest, steps)
    want = jnp.where(place < block, step * step_rows + place * conv + which, -1)
    spread_v[...] = one_hot(lax.broadcasted_iota(jnp.int32, spread_v.shape, 1), want)
    line = lax.broadcasted_iota(jnp.int32, (1, conv * tall), 1)
    rest, place = split_index(line, PADDED)
    which, step = split_index(rest, steps)
    want = jnp.where(place < block, step * step_rows + place * conv + which, -1)
    gather_v[...] = one_hot(lax.broadcasted_iota(jnp.int32, gather_v.shape, 0), want)

    perm_rows = perm_v.shape[0] // 8

    def make_perm(i, carry):
        line = lax.broadcasted_iota(jnp.int32, (perm_rows, 1), 0) + i * perm_rows
        rest, slot = split_index(line, peer_rows)
        rest, quarter = split_index(rest, quarters)
        peer, step = split_index(rest, steps)
        number = slot * dp_count + peer
        which, place = split_index(number, block)
        source = quarter * rows + step * step_rows + place * conv + which
        want = jnp.where(number < step_rows, source, -1)
        have = lax.broadcasted_iota(jnp.int32, (perm_rows, perm_v.shape[1]), 1)
        perm_v[pl.ds(i * perm_rows, perm_rows), :] = one_hot(have, want)
        return carry

    lax.fori_loop(0, 8, make_perm, 0)

    new_copy.wait()
    for part in range(2):
        extra_v[part] = jnp.dot(
            spread_v[...],
            jnp.concatenate([new_v[s, part] for s in range(steps)], axis=0),
            preferred_element_type=jnp.float32,
        ).astype(jnp.bfloat16)
    query_copy.wait()
    for c in range(head_cols // WIDE):
        lanes = slice(c * WIDE, (c + 1) * WIDE)
        pad_v[:, lanes] = jnp.dot(
            spread_v[...], row_v[:, lanes], preferred_element_type=jnp.float32
        ).astype(jnp.bfloat16)
    residual_copy.start()

    q_rows = group * tall
    scale = HD ** (-0.5) * 1.4426950408889634
    extra_row = lax.broadcasted_iota(jnp.int32, (q_rows, EXTRA), 0)
    extra_col = lax.broadcasted_iota(jnp.int32, (q_rows, EXTRA), 1)
    extra_line = extra_row & (PADDED - 1)
    second = (extra_row & PADDED) != 0
    first_keys = extra_col < PADDED
    own_limit = jnp.where(second == first_keys, -1, extra_line)
    own_limit = jnp.where(extra_col < tall, own_limit, -1)
    from_first = jnp.logical_and(second, first_keys)
    key_line = extra_col & (PADDED - 1)
    cache_col = lax.broadcasted_iota(jnp.int32, (1, ctx), 1)
    tall_line = lax.broadcasted_iota(jnp.int32, (tall, HD), 0)
    weights_each = (2 * chunks) // pairs

    def pair_body(p, carry):
        slot = lax.rem(p, SLOTS)

        @pl.when(p + SLOTS - 1 < pairs)
        def _():
            for copy in pair_copies(p + SLOTS - 1):
                copy.start()

        for w in range(weights_each):
            weight_copy(p * weights_each + w).start()
        for copy in pair_copies(p):
            copy.wait()

        for c in range(2):
            b = p * 2 + c
            at = pl.ds(pl.multiple_of(b * tall, tall), tall)
            k_v[slot, c, ctx : ctx + tall, :] = extra_v[0, at, :]
            v_v[slot, c, ctx : ctx + tall, :] = extra_v[1, at, :]
            took = [accepted_ref[s, me * conv + b] for s in range(steps)]
            keep_v[at, :] = jnp.where(
                (tall_line & (PADDED - 1)) <= jnp.where(tall_line < PADDED, took[0], took[1]),
                1.0,
                0.0,
            ).astype(jnp.bfloat16)
            q_wide = pad_v[at, :]
            for k in range(kv_local):
                lanes = slice(k * HD, (k + 1) * HD)
                q = jnp.concatenate(
                    [
                        q_wide[:, (k * group + h) * HD : (k * group + h + 1) * HD]
                        for h in range(group)
                    ],
                    axis=0,
                )
                scores = lax.dot_general(
                    q,
                    k_v[slot, c, :, lanes],
                    (((1,), (1,)), ((), ())),
                    preferred_element_type=jnp.float32,
                )
                cached = jnp.where(cache_col < length_ref[b], scores[:, :ctx], -jnp.inf)
                limit = jnp.where(from_first, took[0], own_limit)
                extra = jnp.where(key_line <= limit, scores[:, ctx:], -jnp.inf)
                top = jnp.maximum(
                    jnp.max(cached, axis=1, keepdims=True), jnp.max(extra, axis=1, keepdims=True)
                )
                top = top * scale
                cached = jnp.exp2(cached * scale - top)
                extra = jnp.exp2(extra * scale - top)
                total = jnp.sum(cached, axis=1, keepdims=True) + jnp.sum(
                    extra, axis=1, keepdims=True
                )
                inverse = 1.0 / total
                weights = jnp.concatenate([cached * inverse, extra * inverse], axis=1)
                result = jnp.dot(
                    weights.astype(jnp.bfloat16),
                    v_v[slot, c, :, lanes],
                    preferred_element_type=jnp.float32,
                ).astype(jnp.bfloat16)
                for h in range(group):
                    head = (k * group + h) * HD
                    pad_v[at, head : head + HD] = result[h * tall : (h + 1) * tall]
        return carry

    lax.fori_loop(0, pairs, pair_body, 0)
    for half in range(2):
        draft_copy(half).start()

    for c in range(head_cols // WIDE):
        lanes = slice(c * WIDE, (c + 1) * WIDE)
        row_v[:, lanes] = jnp.dot(
            gather_v[...], pad_v[:, lanes], preferred_element_type=jnp.float32
        ).astype(jnp.bfloat16)
    pl.semaphore_wait(barrier, dp_count)

    def partial_copy(c):
        slot = lax.rem(c, SENDS)
        return pltpu.make_async_remote_copy(
            src_ref=send_v.at[slot],
            dst_ref=recv_v.at[c],
            send_sem=send_sem.at[slot],
            recv_sem=recv_sem.at[c],
            device_id=(me, other),
            device_id_type=MESH,
        )

    def send_side(c, carry):
        weight_copy(c).wait()
        partial = jnp.dot(row_v[...], weight_v[c], preferred_element_type=jnp.float32)

        @pl.when(c >= SENDS)
        def _():
            partial_copy(c - SENDS).wait_send()

        send_v[lax.rem(c, SENDS)] = partial
        partial_copy(c).start()
        return carry

    lax.fori_loop(0, chunks, send_side, 0)
    square_v[...] = jnp.zeros(square_v.shape, jnp.float32)
    residual_copy.wait()

    def own_side(c, carry):
        weight_copy(c + chunks).wait()
        own = jnp.dot(row_v[...], weight_v[c + chunks], preferred_element_type=jnp.float32)
        at = pl.ds(pl.multiple_of(c * WIDE, WIDE), WIDE)
        own += hidden_v[:, at].astype(jnp.float32)
        partial_copy(c).wait_recv()
        hidden = (own + recv_v[c]).astype(jnp.bfloat16).astype(jnp.float32)
        squares = hidden * hidden
        part = square_v[...]
        for j in range(WIDE // HD):
            part += squares[:, j * HD : (j + 1) * HD]
        square_v[...] = part
        hidden_v[:, at] = (hidden * gain_ref[:, at]).astype(jnp.bfloat16)
        return carry

    lax.fori_loop(0, chunks, own_side, 0)

    def exchange(src, dst, n):
        return pltpu.make_async_remote_copy(
            src_ref=src,
            dst_ref=dst,
            send_sem=ex_send_sem.at[n],
            recv_sem=ex_recv_sem.at[n],
            device_id=(me, other),
            device_id_type=MESH,
        )

    square_copy = exchange(square_v, square_recv, 0)
    square_copy.start()
    draft_copy(0).wait()
    ex_send[...] = jnp.dot(hidden_v[...], draft_v[0], preferred_element_type=jnp.float32)
    draft_out = exchange(ex_send, ex_recv, 1)
    draft_out.start()
    draft_copy(1).wait()
    projected = jnp.dot(hidden_v[...], draft_v[1], preferred_element_type=jnp.float32)
    kept = jnp.dot(gather_v[...], keep_v[...], preferred_element_type=jnp.float32)
    square_copy.wait_recv()
    total = jnp.sum(square_v[...] + square_recv[...], axis=1, keepdims=True)
    factor = lax.rsqrt(total * (1.0 / width) + 1e-05)
    draft_out.wait_recv()
    projected = (projected + ex_recv[...]) * factor
    for j in range(quarters):
        piece = projected[:, j * HD : (j + 1) * HD]
        rows_v[j * rows : (j + 1) * rows, :] = jnp.where(kept > 0.5, piece, 0.0).astype(
            jnp.bfloat16
        )
    packets = jnp.dot(perm_v[...], rows_v[...], preferred_element_type=jnp.float32)
    packet_v[...] = packets.astype(jnp.bfloat16).reshape(packet_v.shape)

    def row_copy(src, dst, peer):
        return pltpu.make_async_remote_copy(
            src_ref=src,
            dst_ref=dst,
            send_sem=row_send_sem,
            recv_sem=row_recv_sem,
            device_id=(peer, core),
            device_id_type=MESH,
        )

    def scatter(k, carry):
        peer = lax.rem(me + k, dp_count)
        row_copy(packet_v.at[peer], out_ref.at[me], peer).start()
        return carry

    lax.fori_loop(1, dp_count, scatter, 0)
    out_ref[me] = packet_v[me]

    for c in range(max(0, chunks - SENDS), chunks):
        partial_copy(c).wait_send()
    square_copy.wait_send()
    draft_out.wait_send()
    most = pl.ds(0, dp_count - 1)
    everything = row_copy(packet_v.at[most], out_ref.at[most], other)
    everything.wait_send()
    everything.wait_recv()


def body(
    queries, new_kv, kv_cache, context_len, accepted, residual, out_weight, draft_gain, draft_weight
):
    dp_count = lax.axis_size("dp")
    steps, conv, block, head_cols = queries.shape
    ctx, kv_cols = kv_cache.shape[2:]
    d_cols = residual.shape[3]
    width = out_weight.shape[1]
    own_cols = draft_weight.shape[1] // 2
    quarters = own_cols // HD
    rows = steps * conv * block
    padded = steps * conv * PADDED
    peer_rows = -(-(conv * block) // dp_count)
    packet = steps * quarters * peer_rows
    chunks = d_cols // WIDE
    anywhere = pl.BlockSpec(memory_space=pl.ANY)
    smem = pl.BlockSpec(memory_space=pltpu.SMEM)
    vmem = pl.BlockSpec(memory_space=pltpu.VMEM)
    bf16, f32 = jnp.bfloat16, jnp.float32
    received = pl.pallas_call(
        functools.partial(fused_kernel, width=width, steps=steps, conv=conv, block=block),
        out_shape=jax.ShapeDtypeStruct((dp_count, packet, HD), bf16),
        in_specs=[smem, smem, vmem] + [anywhere] * 6,
        out_specs=vmem,
        scratch_shapes=[
            pltpu.VMEM((rows, head_cols), bf16),
            pltpu.VMEM((padded, head_cols), bf16),
            pltpu.VMEM((steps, 2, conv * block, kv_cols), bf16),
            pltpu.VMEM((2, padded, kv_cols), bf16),
            pltpu.VMEM((SLOTS, 2, ctx + EXTRA, kv_cols), bf16),
            pltpu.VMEM((SLOTS, 2, ctx + EXTRA, kv_cols), bf16),
            pltpu.VMEM((rows, d_cols), bf16),
            pltpu.VMEM((2 * chunks, head_cols, WIDE), bf16),
            pltpu.VMEM((2, d_cols, own_cols), bf16),
            pltpu.VMEM((padded, rows), bf16),
            pltpu.VMEM((rows, padded), bf16),
            pltpu.VMEM((dp_count * packet, quarters * rows), bf16),
            pltpu.VMEM((padded, HD), bf16),
            pltpu.VMEM((SENDS, rows, WIDE), f32),
            pltpu.VMEM((chunks, rows, WIDE), f32),
            pltpu.VMEM((rows, HD), f32),
            pltpu.VMEM((rows, HD), f32),
            pltpu.VMEM((rows, own_cols), f32),
            pltpu.VMEM((rows, own_cols), f32),
            pltpu.VMEM((quarters * rows, HD), bf16),
            pltpu.VMEM((dp_count, packet, HD), bf16),
            pltpu.SemaphoreType.DMA((3,)),
            pltpu.SemaphoreType.DMA((2, SLOTS)),
            pltpu.SemaphoreType.DMA((2 * chunks,)),
            pltpu.SemaphoreType.DMA((2,)),
            pltpu.SemaphoreType.DMA((SENDS,)),
            pltpu.SemaphoreType.DMA((chunks,)),
            pltpu.SemaphoreType.DMA((2,)),
            pltpu.SemaphoreType.DMA((2,)),
            pltpu.SemaphoreType.DMA,
            pltpu.SemaphoreType.DMA,
        ],
        compiler_params=pltpu.CompilerParams(
            collective_id=0, has_side_effects=True, vmem_limit_bytes=67043328
        ),
        name="verify_and_draft",
    )(
        context_len,
        accepted,
        draft_gain.reshape(1, d_cols),
        queries.transpose(0, 2, 1, 3).reshape(rows, head_cols),
        new_kv.transpose(0, 1, 3, 2, 4).reshape(steps, 2, conv * block, kv_cols),
        kv_cache,
        residual.transpose(0, 2, 1, 3).reshape(rows, d_cols),
        out_weight,
        draft_weight,
    )
    by_slot = received.reshape(dp_count, steps, quarters, peer_rows, HD)
    return by_slot.transpose(1, 0, 3, 2, 4).reshape(steps, dp_count * peer_rows, own_cols)


def solution(mesh):
    in_specs = (
        P(None, "dp", None, "tensor"),
        P(None, None, "dp", None, "tensor"),
        P(None, "dp", None, "tensor"),
        P("dp"),
        P(),
        P(None, "dp", None, "tensor"),
        P("tensor", None),
        P("tensor"),
        P("tensor", None),
    )
    out_specs = P(None, "dp", "tensor")
    return jax.shard_map(body, mesh=mesh, in_specs=in_specs, out_specs=out_specs, check_vma=False)
```

time: 213 us -> 49.8 us (0.23)
  other arithmetic: 52.8 us -> 0 us
  matrix products: 52.4 us -> 0 us
  local copies, waits for them, and re-layouts: 52.4 us -> 1.84 us
  Pallas kernels: 0 us -> 47.7 us
  waiting for transfers between devices: 18.5 us -> 0 us
  starting transfers between devices: 17.1 us -> 0 us
  between operations: 13.6 us -> 0.01 us
  blocking collectives: 5.16 us -> 0 us
    dot_general x8 -> x0, matrix products: 52.4 us -> none  [the longest x2 29.6 us: body(): jnp.dot(attended, out_weight, preferred_element_type=jnp.float32)]
    pallas_call x0 -> x1, Pallas kernels: none -> 47.7 us  [body(): pl.pallas_call(functools.partial(fused_kernel, width=width, steps=steps,...]
    sub x2 -> x0, other arithmetic: 40.5 us -> none  [attend_block(): expons = jnp.exp(scores - maximum)]
    all_to_all x2 -> x0, starting transfers between devices: 16.8 us -> none  [body(): lax.all_to_all(spread_rows(hidden, dp_count, peer_rows), 'dp', split_axis...]
    all_to_all x2 -> x0, waiting for transfers between devices: 15.6 us -> none  [body(): lax.all_to_all(spread_rows(hidden, dp_count, peer_rows), 'dp', split_axis...]
    unnamed x16 -> x0, local copies, waits for them, and re-layouts: 14.4 us -> none
    concatenate x13 -> x0, local copies, waits for them, and re-layouts: 13.1 us -> none  [the longest x5 6.56 us: body(): jnp.concatenate([kv_cache[0], earlier_keys, new_kv[step_index, 0]], axis=1)]
    convert_element_type x8 -> x0, local copies, waits for them, and re-layouts: 9.84 us -> none  [the longest x4 6.68 us: body(): residual[step_index].reshape(row_total, d_cols).astype(jnp.float32) + summed]
  transfers between devices with their start and end apart: 6 -> 0, of which waited for: 3 -> 0; matrix products, arithmetic and copies ran while one was open for 37% -> 0% of each run, Pallas kernels for 0% -> 0%
where the time goes in v1:
time: 49.8 us; the launch traced here: 49.6 us
  Pallas kernels  47.7 us (96%)
  local copies, waits for them, and re-layouts  1.84 us (4%)
    pallas_call x1, Pallas kernels, body(): pl.pallas_call(functools.partial(fused_kernel, width=width, steps=steps,...  47.7 us
    transpose x1, local copies, waits for them, and re-layouts, body(): by_slot.transpose(1, 0, 3, 2, 4)  1.04 us

profile of v1, /device:TPU:1, one launch (start us, length us, event | category | flops | bytes accessed | tf_op | source)
XLA Modules:
  0.0 49.6 jit_solution(584478203556330917)
XLA Ops:
  0.0 47.7 %verify_and_draft.1 = bf16[64,16,128]{2,1,0:T(8,128)(2,1)} custom-call(s32[16]{0:T(128)} %length_ref.1, s32[2,1024]{1,0:T(2,128)} %accepted_ref.1, f32[1,4096]{1,0:T(1,128)} %bitcast.17, bf16[224,2048]{1,0:T(8,128)(2,1)} %bitcast.15, bf16[2,2,112,256]{3,2,1,0:T(8,128)(2,1)} %bitcast.16, bf16[2,16,512,256]{3,2,1,0:T(8,128)(2,1)} %cache_hbm.1, ...), custom_call_target="tpu_custom_call" | custom-call | tf_op jit(solution)/shard_map/verify_and_draft/pallas_call | solution.py:403
  47.7 1.0 %copy.10 = bf16[2,64,2,4,128]{4,3,2,1,0:T(4,128)(2,1)S(1)} copy(bf16[2,64,2,4,128]{4,2,3,0,1:T(2,128)(2,1)} %bitcast.14) | data formatting | bytes 524288 | tf_op jit(solution)/shard_map/transpose | solution.py:457
  48.8 0.8 %reshape.23 = bf16[2,128,512]{2,1,0:T(8,128)(2,1)} reshape(bf16[2,64,2,4,128]{4,3,2,1,0:T(4,128)(2,1)S(1)} %copy.10) | data formatting | bytes 524288 | tf_op jit(solution)/shard_map/reshape | solution.py:457

commit v2 on v1

--- a/solution.py
+++ b/solution.py
@@ -60,7 +60,6 @@
     square_recv,
     ex_send,
     ex_recv,
-    rows_v,
     packet_v,
     first_sem,
     pair_sem,
@@ -78,7 +77,7 @@
     conv,
     block,
 ):
-    dp_count = out_ref.shape[0]
+    dp_count = packet_v.shape[0]
     ctx = cache_hbm.shape[2]
     head_cols = queries_hbm.shape[1]
     kv_local = cache_hbm.shape[3] // HD
@@ -90,7 +89,8 @@
     tall = steps * PADDED
     own_cols = draft_v.shape[2]
     quarters = own_cols // HD
-    peer_rows = packet_v.shape[1] // (steps * quarters)
+    peer_rows = packet_v.shape[3]
+    fold = out_ref.shape[3]
     me = lax.axis_index("dp")
     core = lax.axis_index("tensor")
     other = 1 - core
@@ -155,22 +155,13 @@
     want = jnp.where(place < block, step * step_rows + place * conv + which, -1)
     gather_v[...] = one_hot(lax.broadcasted_iota(jnp.int32, gather_v.shape, 0), want)
 
-    perm_rows = perm_v.shape[0] // 8
-
-    def make_perm(i, carry):
-        line = lax.broadcasted_iota(jnp.int32, (perm_rows, 1), 0) + i * perm_rows
-        rest, slot = split_index(line, peer_rows)
-        rest, quarter = split_index(rest, quarters)
-        peer, step = split_index(rest, steps)
-        number = slot * dp_count + peer
-        which, place = split_index(number, block)
-        source = quarter * rows + step * step_rows + place * conv + which
-        want = jnp.where(number < step_rows, source, -1)
-        have = lax.broadcasted_iota(jnp.int32, (perm_rows, perm_v.shape[1]), 1)
-        perm_v[pl.ds(i * perm_rows, perm_rows), :] = one_hot(have, want)
-        return carry
-
-    lax.fori_loop(0, 8, make_perm, 0)
+    line = lax.broadcasted_iota(jnp.int32, (perm_v.shape[0], 1), 0)
+    rest, slot = split_index(line, peer_rows)
+    peer, step = split_index(rest, steps)
+    number = slot * dp_count + peer
+    which, place = split_index(number, block)
+    want = jnp.where(number < step_rows, step * step_rows + place * conv + which, -1)
+    perm_v[...] = one_hot(lax.broadcasted_iota(jnp.int32, perm_v.shape, 1), want)
 
     new_copy.wait()
     for part in range(2):
@@ -345,13 +336,12 @@
     factor = lax.rsqrt(total * (1.0 / width) + 1e-05)
     draft_out.wait_recv()
     projected = (projected + ex_recv[...]) * factor
+    new_rows = jnp.where(kept[:, :1] > 0.5, projected, 0.0).astype(jnp.bfloat16)
+    packets = jnp.dot(perm_v[...], new_rows, preferred_element_type=jnp.float32)
+    packets = packets.astype(jnp.bfloat16)
     for j in range(quarters):
-        piece = projected[:, j * HD : (j + 1) * HD]
-        rows_v[j * rows : (j + 1) * rows, :] = jnp.where(kept > 0.5, piece, 0.0).astype(
-            jnp.bfloat16
-        )
-    packets = jnp.dot(perm_v[...], rows_v[...], preferred_element_type=jnp.float32)
-    packet_v[...] = packets.astype(jnp.bfloat16).reshape(packet_v.shape)
+        piece = packets[:, j * HD : (j + 1) * HD]
+        packet_v[:, :, j] = piece.reshape(dp_count, steps, peer_rows, HD)
 
     def row_copy(src, dst, peer):
         return pltpu.make_async_remote_copy(
@@ -363,20 +353,23 @@
             device_id_type=MESH,
         )
 
-    def scatter(k, carry):
-        peer = lax.rem(me + k, dp_count)
-        row_copy(packet_v.at[peer], out_ref.at[me], peer).start()
-        return carry
-
-    lax.fori_loop(1, dp_count, scatter, 0)
-    out_ref[me] = packet_v[me]
+    side = round(dp_count ** (1 / 3))
+    digits = [[lax.rem(me // side**a + d, side) * side**a for d in range(side)] for a in range(3)]
+    hops = [min(d, side - d) for d in range(side)]
+    offsets = [(a, b, c) for a in range(side) for b in range(side) for c in range(side)]
+    offsets.sort(key=lambda o: -sum(hops[d] for d in o))
+    top, low = me // fold, lax.rem(me, fold)
+    for a, b, c in offsets[:-1]:
+        peer = digits[2][a] + digits[1][b] + digits[0][c]
+        row_copy(packet_v.at[peer], out_ref.at[:, top, :, low], peer).start()
+    out_ref[:, top, :, low] = packet_v[me]
 
     for c in range(max(0, chunks - SENDS), chunks):
         partial_copy(c).wait_send()
     square_copy.wait_send()
     draft_out.wait_send()
     most = pl.ds(0, dp_count - 1)
-    everything = row_copy(packet_v.at[most], out_ref.at[most], other)
+    everything = row_copy(packet_v.at[most], packet_v.at[most], other)
     everything.wait_send()
     everything.wait_recv()
 
@@ -394,7 +387,7 @@
     rows = steps * conv * block
     padded = steps * conv * PADDED
     peer_rows = -(-(conv * block) // dp_count)
-    packet = steps * quarters * peer_rows
+    fold = 8 // peer_rows
     chunks = d_cols // WIDE
     anywhere = pl.BlockSpec(memory_space=pl.ANY)
     smem = pl.BlockSpec(memory_space=pltpu.SMEM)
@@ -402,7 +395,9 @@
     bf16, f32 = jnp.bfloat16, jnp.float32
     received = pl.pallas_call(
         functools.partial(fused_kernel, width=width, steps=steps, conv=conv, block=block),
-        out_shape=jax.ShapeDtypeStruct((dp_count, packet, HD), bf16),
+        out_shape=jax.ShapeDtypeStruct(
+            (steps, dp_count // fold, quarters, fold, peer_rows, HD), bf16
+        ),
         in_specs=[smem, smem, vmem] + [anywhere] * 6,
         out_specs=vmem,
         scratch_shapes=[
@@ -417,7 +412,7 @@
             pltpu.VMEM((2, d_cols, own_cols), bf16),
             pltpu.VMEM((padded, rows), bf16),
             pltpu.VMEM((rows, padded), bf16),
-            pltpu.VMEM((dp_count * packet, quarters * rows), bf16),
+            pltpu.VMEM((dp_count * steps * peer_rows, rows), bf16),
             pltpu.VMEM((padded, HD), bf16),
             pltpu.VMEM((SENDS, rows, WIDE), f32),
             pltpu.VMEM((chunks, rows, WIDE), f32),
@@ -425,8 +420,7 @@
             pltpu.VMEM((rows, HD), f32),
             pltpu.VMEM((rows, own_cols), f32),
             pltpu.VMEM((rows, own_cols), f32),
-            pltpu.VMEM((quarters * rows, HD), bf16),
-            pltpu.VMEM((dp_count, packet, HD), bf16),
+            pltpu.VMEM((dp_count, steps, quarters, peer_rows, HD), bf16),
             pltpu.SemaphoreType.DMA((3,)),
             pltpu.SemaphoreType.DMA((2, SLOTS)),
             pltpu.SemaphoreType.DMA((2 * chunks,)),
@@ -453,8 +447,8 @@
         out_weight,
         draft_weight,
     )
-    by_slot = received.reshape(dp_count, steps, quarters, peer_rows, HD)
-    return by_slot.transpose(1, 0, 3, 2, 4).reshape(steps, dp_count * peer_rows, own_cols)
+    by_row = received.transpose(0, 1, 3, 4, 2, 5)
+    return by_row.reshape(steps, dp_count * peer_rows, own_cols)
 
 
 def solution(mesh):

time: 49.8 us -> 49.2 us (0.988)
    unnamed x0 -> x1, local copies, waits for them, and re-layouts: none -> 1.67 us
    transpose x1 -> x0, local copies, waits for them, and re-layouts: 1.04 us -> none  [body(): by_slot.transpose(1, 0, 3, 2, 4)]
    reshape x1 -> x0, local copies, waits for them, and re-layouts: 0.8 us -> none  [body(): by_slot.transpose(1, 0, 3, 2, 4)]
where the time goes in v2:
time: 49.2 us; the launch traced here: 49 us
  Pallas kernels  47.3 us (96%)
  local copies, waits for them, and re-layouts  1.67 us (3%)
    pallas_call x1, Pallas kernels, body(): pl.pallas_call(functools.partial(fused_kernel, width=width, steps=steps,...  47.3 us
    unnamed x1, local copies, waits for them, and re-layouts  1.67 us

profile of v2, /device:TPU:1, one launch (start us, length us, event | category | flops | bytes accessed | tf_op | source)
XLA Modules:
  0.0 49.0 jit_solution(15264343278986348179)
XLA Ops:
  0.0 47.3 %verify_and_draft.1 = bf16[2,16,4,4,2,128]{5,4,3,2,1,0:T(2,128)(2,1)} custom-call(s32[16]{0:T(128)} %length_ref.1, s32[2,1024]{1,0:T(2,128)} %accepted_ref.1, f32[1,4096]{1,0:T(1,128)} %bitcast.17, bf16[224,2048]{1,0:T(8,128)(2,1)} %bitcast.15, bf16[2,2,112,256]{3,2,1,0:T(8,128)(2,1)} %bitcast.16, bf16[2,16,512,256]{3,2,1,0:T(8,128)(2,1)} %cache_hbm.1, ...), custom_call_target="tpu_custom_call" | custom-call | tf_op jit(solution)/shard_map/verify_and_draft/pallas_call | solution.py:396
  47.3 1.7 %copy.11 = bf16[2,128,512]{2,1,0:T(8,128)(2,1)} copy(bf16[2,128,512]{2,1,0:T(8,128)(2,1)} %bitcast.14) | data formatting | bytes 524288

commit v3 on v2

--- a/solution.py
+++ b/solution.py
@@ -206,6 +206,7 @@
         for copy in pair_copies(p):
             copy.wait()
 
+        units = []
         for c in range(2):
             b = p * 2 + c
             at = pl.ds(pl.multiple_of(b * tall, tall), tall)
@@ -217,44 +218,56 @@
                 1.0,
                 0.0,
             ).astype(jnp.bfloat16)
+            limit = jnp.where(from_first, took[0], own_limit)
             q_wide = pad_v[at, :]
             for k in range(kv_local):
-                lanes = slice(k * HD, (k + 1) * HD)
-                q = jnp.concatenate(
-                    [
-                        q_wide[:, (k * group + h) * HD : (k * group + h + 1) * HD]
-                        for h in range(group)
-                    ],
-                    axis=0,
-                )
-                scores = lax.dot_general(
-                    q,
-                    k_v[slot, c, :, lanes],
-                    (((1,), (1,)), ((), ())),
-                    preferred_element_type=jnp.float32,
-                )
-                cached = jnp.where(cache_col < length_ref[b], scores[:, :ctx], -jnp.inf)
-                limit = jnp.where(from_first, took[0], own_limit)
-                extra = jnp.where(key_line <= limit, scores[:, ctx:], -jnp.inf)
-                top = jnp.maximum(
-                    jnp.max(cached, axis=1, keepdims=True), jnp.max(extra, axis=1, keepdims=True)
-                )
-                top = top * scale
-                cached = jnp.exp2(cached * scale - top)
-                extra = jnp.exp2(extra * scale - top)
-                total = jnp.sum(cached, axis=1, keepdims=True) + jnp.sum(
-                    extra, axis=1, keepdims=True
-                )
-                inverse = 1.0 / total
-                weights = jnp.concatenate([cached * inverse, extra * inverse], axis=1)
-                result = jnp.dot(
-                    weights.astype(jnp.bfloat16),
-                    v_v[slot, c, :, lanes],
-                    preferred_element_type=jnp.float32,
-                ).astype(jnp.bfloat16)
-                for h in range(group):
-                    head = (k * group + h) * HD
-                    pad_v[at, head : head + HD] = result[h * tall : (h + 1) * tall]
+                units.append((c, k, at, cache_col < length_ref[b], key_line <= limit, q_wide))
+
+        def score(unit):
+            c, k, _, _, _, q_wide = unit
+            q = jnp.concatenate(
+                [q_wide[:, (k * group + h) * HD : (k * group + h + 1) * HD] for h in range(group)],
+                axis=0,
+            )
+            return lax.dot_general(
+                q,
+                k_v[slot, c, :, k * HD : (k + 1) * HD],
+                (((1,), (1,)), ((), ())),
+                preferred_element_type=jnp.float32,
+            )
+
+        def attend(unit, scores):
+            c, k, _, valid, allowed, _ = unit
+            cached = jnp.where(valid, scores[:, :ctx], -jnp.inf)
+            extra = jnp.where(allowed, scores[:, ctx:], -jnp.inf)
+            top = jnp.maximum(
+                jnp.max(cached, axis=1, keepdims=True), jnp.max(extra, axis=1, keepdims=True)
+            )
+            top = top * scale
+            cached = jnp.exp2(cached * scale - top)
+            extra = jnp.exp2(extra * scale - top)
+            total = jnp.sum(cached, axis=1, keepdims=True) + jnp.sum(extra, axis=1, keepdims=True)
+            inverse = 1.0 / total
+            weights = jnp.concatenate([cached * inverse, extra * inverse], axis=1)
+            result = jnp.dot(
+                weights.astype(jnp.bfloat16),
+                v_v[slot, c, :, k * HD : (k + 1) * HD],
+                preferred_element_type=jnp.float32,
+            )
+            return result.astype(jnp.bfloat16)
+
+        results = []
+        ahead = score(units[0])
+        for n, unit in enumerate(units):
+            scores = ahead
+            if n + 1 < len(units):
+                ahead = score(units[n + 1])
+            results.append(attend(unit, scores))
+        for unit, result in zip(units, results):
+            _, k, at, _, _, _ = unit
+            for h in range(group):
+                head = (k * group + h) * HD
+                pad_v[at, head : head + HD] = result[h * tall : (h + 1) * tall]
         return carry
 
     lax.fori_loop(0, pairs, pair_body, 0)

time: 49.2 us -> 45.1 us (0.917)
  Pallas kernels: 47.3 us -> 43.3 us
    pallas_call x1, Pallas kernels: 47.3 us -> 43.3 us  [body(): pl.pallas_call(functools.partial(fused_kernel, width=width, steps=steps,...]
where the time goes in v3:
time: 45.1 us; the launch traced here: 44.9 us
  Pallas kernels  43.3 us (96%)
  local copies, waits for them, and re-layouts  1.67 us (4%)
    pallas_call x1, Pallas kernels, body(): pl.pallas_call(functools.partial(fused_kernel, width=width, steps=steps,...  43.3 us
    unnamed x1, local copies, waits for them, and re-layouts  1.67 us

profile of v3, /device:TPU:1, one launch (start us, length us, event | category | flops | bytes accessed | tf_op | source)
XLA Modules:
  0.0 44.9 jit_solution(771704235272370640)
XLA Ops:
  0.0 43.3 %verify_and_draft.1 = bf16[2,16,4,4,2,128]{5,4,3,2,1,0:T(2,128)(2,1)} custom-call(s32[16]{0:T(128)} %length_ref.1, s32[2,1024]{1,0:T(2,128)} %accepted_ref.1, f32[1,4096]{1,0:T(1,128)} %bitcast.17, bf16[224,2048]{1,0:T(8,128)(2,1)} %bitcast.15, bf16[2,2,112,256]{3,2,1,0:T(8,128)(2,1)} %bitcast.16, bf16[2,16,512,256]{3,2,1,0:T(8,128)(2,1)} %cache_hbm.1, ...), custom_call_target="tpu_custom_call" | custom-call | tf_op jit(solution)/shard_map/verify_and_draft/pallas_call | solution.py:409
  43.3 1.7 %copy.11 = bf16[2,128,512]{2,1,0:T(8,128)(2,1)} copy(bf16[2,128,512]{2,1,0:T(8,128)(2,1)} %bitcast.14) | data formatting | bytes 524288

commit v4 on v3

--- a/solution.py
+++ b/solution.py
@@ -11,7 +11,9 @@
 PADDED = 8
 EXTRA = 128
 SLOTS = 3
+GROUP = 2
 SENDS = 4
+AHEAD = 2
 WIDE = 512
 MESH = pl.DeviceIdType.MESH
 
@@ -82,7 +84,7 @@
     head_cols = queries_hbm.shape[1]
     kv_local = cache_hbm.shape[3] // HD
     group = head_cols // HD // kv_local
-    pairs = conv // 2
+    pairs = conv // GROUP
     chunks = recv_v.shape[0]
     step_rows = conv * block
     rows = steps * step_rows
@@ -97,7 +99,7 @@
 
     def pair_copies(p):
         slot = lax.rem(p, SLOTS)
-        span = pl.ds(p * 2, 2)
+        span = pl.ds(p * GROUP, GROUP)
         return (
             pltpu.make_async_copy(
                 cache_hbm.at[0, span], k_v.at[slot, :, pl.ds(0, ctx)], pair_sem.at[0, slot]
@@ -141,8 +143,8 @@
 
     lax.fori_loop(1, dp_count, greet, 0)
 
-    k_v[:, :, ctx + tall :, :] = jnp.zeros((SLOTS, 2, EXTRA - tall, kv_local * HD), jnp.bfloat16)
-    v_v[:, :, ctx + tall :, :] = jnp.zeros((SLOTS, 2, EXTRA - tall, kv_local * HD), jnp.bfloat16)
+    k_v[:, :, ctx + tall :, :] = jnp.zeros((SLOTS, GROUP, EXTRA - tall, kv_local * HD), jnp.bfloat16)
+    v_v[:, :, ctx + tall :, :] = jnp.zeros((SLOTS, GROUP, EXTRA - tall, kv_local * HD), jnp.bfloat16)
 
     line = lax.broadcasted_iota(jnp.int32, (conv * tall, 1), 0)
     rest, place = split_index(line, PADDED)
@@ -201,14 +203,17 @@
             for copy in pair_copies(p + SLOTS - 1):
                 copy.start()
 
-        for w in range(weights_each):
-            weight_copy(p * weights_each + w).start()
+        @pl.when(p >= 1)
+        def _():
+            for w in range(weights_each):
+                weight_copy((p - 1) * weights_each + w).start()
+
         for copy in pair_copies(p):
             copy.wait()
 
         units = []
-        for c in range(2):
-            b = p * 2 + c
+        for c in range(GROUP):
+            b = p * GROUP + c
             at = pl.ds(pl.multiple_of(b * tall, tall), tall)
             k_v[slot, c, ctx : ctx + tall, :] = extra_v[0, at, :]
             v_v[slot, c, ctx : ctx + tall, :] = extra_v[1, at, :]
@@ -257,12 +262,11 @@
             return result.astype(jnp.bfloat16)
 
         results = []
-        ahead = score(units[0])
+        ahead = [score(unit) for unit in units[:AHEAD]]
         for n, unit in enumerate(units):
-            scores = ahead
-            if n + 1 < len(units):
-                ahead = score(units[n + 1])
-            results.append(attend(unit, scores))
+            if n + AHEAD < len(units):
+                ahead.append(score(units[n + AHEAD]))
+            results.append(attend(unit, ahead[n]))
         for unit, result in zip(units, results):
             _, k, at, _, _, _ = unit
             for h in range(group):
@@ -271,6 +275,8 @@
         return carry
 
     lax.fori_loop(0, pairs, pair_body, 0)
+    for w in range(weights_each):
+        weight_copy((pairs - 1) * weights_each + w).start()
     for half in range(2):
         draft_copy(half).start()
 
@@ -418,8 +424,8 @@
             pltpu.VMEM((padded, head_cols), bf16),
             pltpu.VMEM((steps, 2, conv * block, kv_cols), bf16),
             pltpu.VMEM((2, padded, kv_cols), bf16),
-            pltpu.VMEM((SLOTS, 2, ctx + EXTRA, kv_cols), bf16),
-            pltpu.VMEM((SLOTS, 2, ctx + EXTRA, kv_cols), bf16),
+            pltpu.VMEM((SLOTS, GROUP, ctx + EXTRA, kv_cols), bf16),
+            pltpu.VMEM((SLOTS, GROUP, ctx + EXTRA, kv_cols), bf16),
             pltpu.VMEM((rows, d_cols), bf16),
             pltpu.VMEM((2 * chunks, head_cols, WIDE), bf16),
             pltpu.VMEM((2, d_cols, own_cols), bf16),

time: 45.1 us -> 44.4 us (0.984)
  Pallas kernels: 43.3 us -> 42.6 us
    pallas_call x1, Pallas kernels: 43.3 us -> 42.6 us  [body(): pl.pallas_call(functools.partial(fused_kernel, width=width, steps=steps,...]
where the time goes in v4:
time: 44.4 us; the launch traced here: 44.2 us
  Pallas kernels  42.6 us (96%)
  local copies, waits for them, and re-layouts  1.67 us (4%)
    pallas_call x1, Pallas kernels, body(): pl.pallas_call(functools.partial(fused_kernel, width=width, steps=steps,...  42.6 us
    unnamed x1, local copies, waits for them, and re-layouts  1.67 us

profile of v4, /device:TPU:1, one launch (start us, length us, event | category | flops | bytes accessed | tf_op | source)
XLA Modules:
  0.0 44.2 jit_solution(14662191979095336222)
XLA Ops:
  0.0 42.6 %verify_and_draft.1 = bf16[2,16,4,4,2,128]{5,4,3,2,1,0:T(2,128)(2,1)} custom-call(s32[16]{0:T(128)} %length_ref.1, s32[2,1024]{1,0:T(2,128)} %accepted_ref.1, f32[1,4096]{1,0:T(1,128)} %bitcast.17, bf16[224,2048]{1,0:T(8,128)(2,1)} %bitcast.15, bf16[2,2,112,256]{3,2,1,0:T(8,128)(2,1)} %bitcast.16, bf16[2,16,512,256]{3,2,1,0:T(8,128)(2,1)} %cache_hbm.1, ...), custom_call_target="tpu_custom_call" | custom-call | tf_op jit(solution)/shard_map/verify_and_draft/pallas_call | solution.py:415
  42.6 1.7 %copy.11 = bf16[2,128,512]{2,1,0:T(8,128)(2,1)} copy(bf16[2,128,512]{2,1,0:T(8,128)(2,1)} %bitcast.14) | data formatting | bytes 524288
